TPU v7x, 512 devices: a whole 4x4x16 slice. The times are simulated.
512 devices in a mesh: slab: 128 (over x, z, y_hi), head: 4 (over y_lo, core).
Axes of the slice: x: 4, y: 4 (y_hi: 2, y_lo: 2; y = y_hi * 2 + y_lo), z: 16, core: 2. Of those that a mesh axis runs over, the one named last changes fastest.
Arguments:
- query_in: bfloat16 [49152, 3072], P(('slab', 'head')), may hold values from -6 to 6
- key_in: bfloat16 [49152, 3072], P(('slab', 'head')), may hold values from -6 to 6
- value_in: bfloat16 [49152, 3072], P(('slab', 'head')), may hold values from -6 to 6
- grad_out: bfloat16 [49152, 3072], P(('slab', 'head')), may hold values from -6 to 6
- neighbours: int32 [768, 16], P('slab'), may hold values from -1 to 767, as said below
Outputs:
- attended: bfloat16 [49152, 3072], P(('slab', 'head'))
- grad_query: bfloat16 [49152, 3072], P(('slab', 'head'))
- grad_key: bfloat16 [49152, 3072], P(('slab', 'head'))
- grad_value: bfloat16 [49152, 3072], P(('slab', 'head'))
Inputs may be any that keep to these rules, and one draw needn't show every extreme that they name: `neighbours`: slab s is tiles s * 6 to (s + 1) * 6 - 1. Row t names distinct key tiles, all in the slab of tile t or in the slabs directly before and after it; its first entry is t itself; -1 marks an unused slot, which names no tile.
All inputs are finite; a program needn't handle non-finite values.
Results may differ from a plain program's by a relative error of at most 0.018.
Values may be sent and summed in bfloat16 or wider, within the bound.
A program may use at most 64 MiB of HBM per device.

v0:
```python
import math

import jax
import jax.numpy as jnp
from jax import lax
from jax.sharding import PartitionSpec as P

HD = 128
TILE = 64


def shifted(shard, axis, by):
    peers = lax.axis_size(axis)
    pairs = [(i, i + by) for i in range(peers) if 0 <= i + by < peers]
    return lax.ppermute(shard, axis, pairs)


def window_mask(id_rows, first_tile, key_count):
    tiles_key = key_count // TILE
    tile_ids = first_tile + jnp.arange(tiles_key, dtype=jnp.int32)
    listed = jnp.any(
        (id_rows[:, :, None] == tile_ids[None, None, :]) & (id_rows[:, :, None] >= 0), axis=1
    )
    tile_count = id_rows.shape[0]
    spread = jnp.broadcast_to(listed[:, None, :, None], (tile_count, TILE, tiles_key, TILE))
    return spread.reshape(tile_count * TILE, key_count)


def attend_tile(query_tile, grad_tile, id_row, key_win, val_win, first_tile):
    score_scale = 1.0 / math.sqrt(HD)
    head_count = query_tile.shape[1] // HD
    query_heads = query_tile.reshape(-1, head_count, HD)
    grad_heads = grad_tile.reshape(-1, head_count, HD)
    key_heads = key_win.reshape(-1, head_count, HD)
    val_heads = val_win.reshape(-1, head_count, HD)
    allowed = window_mask(id_row[None, :], first_tile, key_win.shape[0])[None]
    scores = (
        jnp.einsum("qhd,khd->hqk", query_heads, key_heads, preferred_element_type=jnp.float32)
        * score_scale
    )
    scores = jnp.where(allowed, scores, -1e30)
    row_peak = jnp.max(scores, axis=2, keepdims=True)
    log_total = row_peak + jnp.log(jnp.sum(jnp.exp(scores - row_peak), axis=2, keepdims=True))
    weights = jnp.where(allowed, jnp.exp(scores - log_total), 0.0)
    weights_low = weights.astype(jnp.bfloat16)
    out_heads = jnp.einsum(
        "hqk,khd->qhd", weights_low, val_heads, preferred_element_type=jnp.float32
    ).astype(jnp.bfloat16)
    out_dot = jnp.sum(grad_heads.astype(jnp.float32) * out_heads.astype(jnp.float32), axis=2)
    dweights = jnp.einsum("qhd,khd->hqk", grad_heads, val_heads, preferred_element_type=jnp.float32)
    dscores = (weights * (dweights - out_dot.T[:, :, None])).astype(jnp.bfloat16)
    dq_heads = (
        jnp.einsum("hqk,khd->qhd", dscores, key_heads, preferred_element_type=jnp.float32)
        * score_scale
    ).astype(jnp.bfloat16)
    return (
        out_heads.reshape(query_tile.shape),
        dq_heads.reshape(query_tile.shape),
        log_total[:, :, 0].T,
        out_dot,
        weights_low,
        dscores,
    )


def per_device(query_in, key_in, value_in, grad_out, neighbours):
    score_scale = 1.0 / math.sqrt(HD)
    local_query, local_key, local_value, local_grad = (
        lax.all_to_all(query_in, "head", split_axis=1, concat_axis=0, tiled=True),
        lax.all_to_all(key_in, "head", split_axis=1, concat_axis=0, tiled=True),
        lax.all_to_all(value_in, "head", split_axis=1, concat_axis=0, tiled=True),
        lax.all_to_all(grad_out, "head", split_axis=1, concat_axis=0, tiled=True),
    )
    slab_rows = local_query.shape[0]
    width_local = local_query.shape[1]
    head_count = width_local // HD
    slab_tiles = neighbours.shape[0]
    own_first = lax.axis_index("slab") * slab_tiles
    joined = jnp.concatenate([local_key, local_value], axis=1)
    beside = {}
    for offset in (1, -1):
        beside[offset] = shifted(joined, "slab", offset)
    window = jnp.concatenate([beside[1], joined, beside[-1]], axis=0)
    key_win = window[:, :width_local]
    val_win = window[:, width_local:]
    first_tile = own_first - slab_tiles
    query_tiles = local_query.reshape(slab_tiles, TILE, width_local)
    grad_tiles = local_grad.reshape(slab_tiles, TILE, width_local)

    def per_tile(pieces):
        return attend_tile(pieces[0], pieces[1], pieces[2], key_win, val_win, first_tile)

    out_tiles, dq_tiles, lse_tiles, dot_tiles, weight_tiles, dscore_tiles = lax.map(
        per_tile, (query_tiles, grad_tiles, neighbours)
    )
    attended = out_tiles.reshape(slab_rows, width_local)
    grad_query = dq_tiles.reshape(slab_rows, width_local)
    query_four = local_query.reshape(slab_tiles, TILE, head_count, HD)
    grad_four = local_grad.reshape(slab_tiles, TILE, head_count, HD)

    def window_grads(low_row, high_row):
        key_part = (
            jnp.einsum(
                "jhqk,jqhd->khd",
                dscore_tiles[..., low_row:high_row],
                query_four,
                preferred_element_type=jnp.float32,
            )
            * score_scale
        )
        value_part = jnp.einsum(
            "jhqk,jqhd->khd",
            weight_tiles[..., low_row:high_row],
            grad_four,
            preferred_element_type=jnp.float32,
        )
        return jnp.concatenate(
            [
                key_part.reshape(high_row - low_row, width_local),
                value_part.reshape(high_row - low_row, width_local),
            ],
            axis=1,
        )

    outgoing = {1: window_grads(2 * slab_rows, 3 * slab_rows), -1: window_grads(0, slab_rows)}
    arrived = {}
    for offset in (1, -1):
        arrived[offset] = shifted(outgoing[offset].astype(jnp.bfloat16), "slab", offset).astype(
            jnp.float32
        )
    own_part = window_grads(slab_rows, 2 * slab_rows)
    grad_sum = own_part + arrived[1] + arrived[-1]
    grad_key = grad_sum[:, :width_local].astype(jnp.bfloat16)
    grad_value = grad_sum[:, width_local:].astype(jnp.bfloat16)
    return (
        lax.all_to_all(attended, "head", split_axis=0, concat_axis=1, tiled=True),
        lax.all_to_all(grad_query, "head", split_axis=0, concat_axis=1, tiled=True),
        lax.all_to_all(grad_key, "head", split_axis=0, concat_axis=1, tiled=True),
        lax.all_to_all(grad_value, "head", split_axis=0, concat_axis=1, tiled=True),
    )


def solution(mesh):
    in_specs = (
        P(("slab", "head"), None),
        P(("slab", "head"), None),
        P(("slab", "head"), None),
        P(("slab", "head"), None),
        P("slab", None),
    )
    out_specs = (
        P(("slab", "head"), None),
        P(("slab", "head"), None),
        P(("slab", "head"), None),
        P(("slab", "head"), None),
    )
    return jax.shard_map(
        per_device, mesh=mesh, in_specs=in_specs, out_specs=out_specs, check_vma=False
    )
```

profile of v0, /device:TPU:22, one launch (start us, length us, event | category | flops | bytes accessed | tf_op | source)
XLA Modules:
  0.0 362.4 jit_solution(1754258630447721684)
XLA Ops:
  0.6 2.0 copy.290
  2.6 3.5 all-to-all-start.1
  6.2 9.4 %all-to-all-done.1 = bf16[96,4,768]{2,0,1:T(8,128)(2,1)S(1)} async-done(((bf16[96,4,768]{2,0,1:T(8,128)(2,1)}), bf16[96,4,768]{2,0,1:T(8,128)(2,1)S(1)}, u32[]{:S(2)}, u32[]{:S(2)}) %all-to-all-start.1) | async-done | bytes 589856 | tf_op jit(solution)/shard_map/all_to_all | solution.py:70
  15.6 12.0 %all_to_all.146 = bf16[96,4,768]{2,0,1:T(8,128)(2,1)S(1)} all-to-all(bf16[96,4,768]{2,0,1:T(8,128)(2,1)S(1)} %bitcast.155), channel_id=1, replica_groups=mesh['slab'=128,'head'=4] {'head'}, dimensions={1} | all-to-all | bytes 1179648 | tf_op jit(solution)/shard_map/all_to_all | solution.py:71
  28.7 3.6 collective-permute-start
  32.3 3.7 %collective-permute-start.1 = (bf16[384,1536]{1,0:T(8,128)(2,1)}, bf16[384,1536]{1,0:T(8,128)(2,1)}, u32[]{:S(2)}, u32[]{:S(2)}) collective-permute-start(bf16[384,1536]{1,0:T(8,128)(2,1)} %pad_maximum_fusion.1), channel_id=1, source_target_pairs={{4,0},{8,4},{12,8},{16,12},{20,16},{24,20},{28,24},{32,28},{36,32}... | collective-permute-start | bytes 3538952 | tf_op jit(solution)/shard_map/ppermute | solution.py:15
  36.9 3.5 all-to-all-start
  40.4 1.9 copy.288
  42.3 51.1 %all-to-all-done = bf16[96,4,768]{2,0,1:T(8,128)(2,1)S(1)} async-done(((bf16[96,4,768]{2,0,1:T(8,128)(2,1)}), bf16[96,4,768]{2,0,1:T(8,128)(2,1)S(1)}, u32[]{:S(2)}, u32[]{:S(2)}) %all-to-all-start) | async-done | bytes 589856 | tf_op jit(solution)/shard_map/all_to_all | solution.py:69
  93.5 3.5 all-to-all-start.3
  98.5 7.9 %all-to-all-done.3 = bf16[96,4,768]{2,0,1:T(8,128)(2,1)S(1)} async-done(((bf16[96,4,768]{2,0,1:T(8,128)(2,1)}), bf16[96,4,768]{2,0,1:T(8,128)(2,1)S(1)}, u32[]{:S(2)}, u32[]{:S(2)}) %all-to-all-start.3) | async-done | bytes 589856 | tf_op jit(solution)/shard_map/all_to_all | solution.py:72
  108.0 2.0 pad_maximum_fusion
  111.5 2.7 copy.217
  114.2 2.2 copy.218
  116.4 130.1 %while.16 = (s32[]{:T(128)}, bf16[6,64,768]{2,1,0:T(8,128)(2,1)}, bf16[6,64,768]{2,1,0:T(8,128)(2,1)}, bf16[6,6,64,1152]{3,2,0,1:T(8,128)(2,1)}, bf16[6,6,64,115...) while((s32[]{:T(128)}, bf16[6,64,768]{2,1,0:T(8,128)(2,1)}, ...), condition=%wide.region_5.6_spmd, body=%wide.region_0.5_spmd.sunk | while | flops 460406912 | bytes 29419984 | solution.py:93
  122.5 1.7 reshape.218
  124.1 3.1 multiply_reduce_fusion.2
  127.2 1.6 bitcast_dynamic-update-slice_fusion.4
  130.3 1.7 broadcast_in_dim.76
  132.0 1.6 copy.301
  133.6 1.7 broadcast_in_dim.77
  135.3 1.6 constant_dynamic-update-slice_fusion.3
  144.2 1.7 reshape.218
  145.9 3.1 multiply_reduce_fusion.2
  152.0 1.7 broadcast_in_dim.76
  155.3 1.7 broadcast_in_dim.77
  157.0 1.6 constant_dynamic-update-slice_fusion.3
  165.9 1.7 reshape.218
  167.5 3.1 multiply_reduce_fusion.2
  173.7 1.7 broadcast_in_dim.76
  175.4 1.6 copy.301
  177.0 1.7 broadcast_in_dim.77
  178.6 1.6 constant_dynamic-update-slice_fusion.3
  187.6 1.7 reshape.218
  189.3 3.1 multiply_reduce_fusion.2
  195.4 1.7 broadcast_in_dim.76
  198.7 1.7 broadcast_in_dim.77
  200.3 1.6 constant_dynamic-update-slice_fusion.3
  209.2 1.7 reshape.218
  210.9 3.1 multiply_reduce_fusion.2
  217.1 1.7 broadcast_in_dim.76
  218.7 1.6 copy.301
  220.3 1.7 broadcast_in_dim.77
  222.0 1.6 constant_dynamic-update-slice_fusion.3
  230.9 1.7 reshape.218
  232.6 3.1 multiply_reduce_fusion.2
  238.7 1.7 broadcast_in_dim.76
  242.0 1.7 broadcast_in_dim.77
  243.7 1.6 constant_dynamic-update-slice_fusion.3
  246.6 2.4 fusion.50
  249.0 3.0 fusion.53
  257.6 1.9 collective-permute-start.2
  263.2 5.4 %collective-permute-start.3 = (bf16[384,1536]{1,0:T(8,128)(2,1)}, bf16[384,1536]{1,0:T(8,128)(2,1)}, u32[]{:S(2)}, u32[]{:S(2)}) collective-permute-start(bf16[384,1536]{1,0:T(8,128)(2,1)} %pad_maximum_fusion.3), channel_id=1, source_target_pairs={{4,0},{8,4},{12,8},{16,12},{20,16},{24,20},{28,24},{32,28},{36,32}... | collective-permute-start | bytes 3538952 | tf_op jit(solution)/shard_map/ppermute | solution.py:15
  268.6 4.4 %all-to-all-start.4 = ((bf16[4,96,768]{2,1,0:T(8,128)(2,1)}), bf16[4,96,768]{2,1,0:T(8,128)(2,1)}, u32[]{:S(2)}, u32[]{:S(2)}) async-start(bf16[4,96,768]{2,1,0:T(8,128)(2,1)} %bitcast.162), calls=%async_computation.4 | async-start | bytes 1179648 | tf_op jit(solution)/shard_map/all_to_all | solution.py:136
  273.0 2.1 fusion.47
  275.5 2.1 fusion.22
  277.9 45.8 %all-to-all-done.4 = bf16[4,96,768]{2,1,0:T(8,128)(2,1)} async-done(((bf16[4,96,768]{2,1,0:T(8,128)(2,1)}), bf16[4,96,768]{2,1,0:T(8,128)(2,1)}, u32[]{:S(2)}, u32[]{:S(2)}) %all-to-all-start.4) | async-done | bytes 589856 | tf_op jit(solution)/shard_map/all_to_all | solution.py:136
  323.7 3.5 all-to-all-start.5
  327.2 2.0 fusion.13
  330.1 6.6 %all-to-all-done.5 = bf16[4,96,768]{2,1,0:T(8,128)(2,1)S(1)} async-done(((bf16[4,96,768]{2,1,0:T(8,128)(2,1)}), bf16[4,96,768]{2,1,0:T(8,128)(2,1)S(1)}, u32[]{:S(2)}, u32[]{:S(2)}) %all-to-all-start.5) | async-done | bytes 589856 | tf_op jit(solution)/shard_map/all_to_all | solution.py:137
  336.7 11.9 %all_to_all.147 = bf16[4,96,768]{2,1,0:T(8,128)(2,1)S(1)} all-to-all(bf16[4,96,768]{2,1,0:T(8,128)(2,1)S(1)} %bitcast.156), channel_id=1, replica_groups=mesh['slab'=128,'head'=4] {'head'}, dimensions={0} | all-to-all | bytes 1179648 | tf_op jit(solution)/shard_map/all_to_all | solution.py:138
  348.5 3.5 all-to-all-start.7
  352.0 1.9 copy.259
  355.7 5.8 %all-to-all-done.7 = bf16[4,96,768]{2,1,0:T(8,128)(2,1)S(1)} async-done(((bf16[4,96,768]{2,1,0:T(8,128)(2,1)}), bf16[4,96,768]{2,1,0:T(8,128)(2,1)S(1)}, u32[]{:S(2)}, u32[]{:S(2)}) %all-to-all-start.7) | async-done | bytes 589856 | tf_op jit(solution)/shard_map/all_to_all | solution.py:139
  (158 shorter events, 85.4 us)
Async XLA Ops:
  0.6 5.5 %copy-start.7 = (bf16[96,3072]{1,0:T(8,128)(2,1)S(1)}, bf16[96,3072]{1,0:T(8,128)(2,1)}, u32[]{:S(2)}) copy-start(bf16[96,3072]{1,0:T(8,128)(2,1)} %param.9) | copy-start | bytes 1769476
  2.6 13.0 %all-to-all-start.1 = ((bf16[96,4,768]{2,0,1:T(8,128)(2,1)}), bf16[96,4,768]{2,0,1:T(8,128)(2,1)S(1)}, u32[]{:S(2)}, u32[]{:S(2)}) async-start(bf16[96,4,768]{2,0,1:T(8,128)(2,1)} %bitcast.115), calls=%async_computation.1 | async-start | bytes 1179648 | tf_op jit(solution)/shard_map/all_to_all | solution.py:70
  15.6 20.5 %copy-start.8 = (bf16[96,3072]{1,0:T(8,128)(2,1)S(1)}, bf16[96,3072]{1,0:T(8,128)(2,1)}, u32[]{:S(2)}) copy-start(bf16[96,3072]{1,0:T(8,128)(2,1)} %param.7) | copy-start | bytes 1769476
  28.7 79.3 %collective-permute-start = (bf16[384,1536]{1,0:T(8,128)(2,1)}, bf16[384,1536]{1,0:T(8,128)(2,1)S(1)}, u32[]{:S(2)}, u32[]{:S(2)}) collective-permute-start(bf16[384,1536]{1,0:T(8,128)(2,1)} %pad_maximum_fusion.1), channel_id=1, source_target_pairs={{0,4},{4,8},{8,12},{12,16},{16,20},{20,24},{24,28},{28,32},{32,36}... | collective-permute-start | bytes 3538952 | tf_op jit(solution)/shard_map/ppermute | solution.py:15
  32.3 75.7 %collective-permute-start.1 = (bf16[384,1536]{1,0:T(8,128)(2,1)}, bf16[384,1536]{1,0:T(8,128)(2,1)}, u32[]{:S(2)}, u32[]{:S(2)}) collective-permute-start(bf16[384,1536]{1,0:T(8,128)(2,1)} %pad_maximum_fusion.1), channel_id=1, source_target_pairs={{4,0},{8,4},{12,8},{16,12},{20,16},{24,20},{28,24},{32,28},{36,32}... | collective-permute-start | bytes 3538952 | tf_op jit(solution)/shard_map/ppermute | solution.py:15
  36.9 56.5 %all-to-all-start = ((bf16[96,4,768]{2,0,1:T(8,128)(2,1)}), bf16[96,4,768]{2,0,1:T(8,128)(2,1)S(1)}, u32[]{:S(2)}, u32[]{:S(2)}) async-start(bf16[96,4,768]{2,0,1:T(8,128)(2,1)} %bitcast.116), calls=%async_computation | async-start | bytes 1179648 | tf_op jit(solution)/shard_map/all_to_all | solution.py:69
  93.5 14.5 %copy-start.2 = (bf16[96,4,768]{2,0,1:T(8,128)(2,1)}, bf16[96,4,768]{2,0,1:T(8,128)(2,1)S(1)}, u32[]{:S(2)}) copy-start(bf16[96,4,768]{2,0,1:T(8,128)(2,1)S(1)} %all-to-all-done) | copy-start | bytes 1769476
  93.5 13.0 %all-to-all-start.3 = ((bf16[96,4,768]{2,0,1:T(8,128)(2,1)}), bf16[96,4,768]{2,0,1:T(8,128)(2,1)S(1)}, u32[]{:S(2)}, u32[]{:S(2)}) async-start(bf16[96,4,768]{2,0,1:T(8,128)(2,1)} %bitcast.113), calls=%async_computation.3 | async-start | bytes 1179648 | tf_op jit(solution)/shard_map/all_to_all | solution.py:72
  106.4 1.6 copy-start.3
  124.1 3.1 copy-start
  124.1 3.1 copy-start.1
  145.9 3.1 copy-start
  145.9 3.1 copy-start.1
  167.5 3.1 copy-start
  167.5 3.1 copy-start.1
  189.3 3.1 copy-start
  189.3 3.1 copy-start.1
  210.9 3.1 copy-start
  210.9 3.1 copy-start.1
  232.6 3.1 copy-start
  232.6 3.1 copy-start.1
  246.6 2.4 copy-start.5
  246.6 5.5 %copy-start.6 = (bf16[6,6,64,1152]{3,2,0,1:T(8,128)(2,1)S(1)}, bf16[6,6,64,1152]{3,2,0,1:T(8,128)(2,1)}, u32[]{:S(2)}) copy-start(bf16[6,6,64,1152]{3,2,0,1:T(8,128)(2,1)} %get-tuple-element.67) | copy-start | bytes 15925252
  249.0 3.0 copy-start.4
  257.6 69.6 %collective-permute-start.2 = (bf16[384,1536]{1,0:T(8,128)(2,1)}, bf16[384,1536]{1,0:T(8,128)(2,1)}, u32[]{:S(2)}, u32[]{:S(2)}) collective-permute-start(bf16[384,1536]{1,0:T(8,128)(2,1)} %pad_maximum_fusion.2), channel_id=1, source_target_pairs={{0,4},{4,8},{8,12},{12,16},{16,20},{20,24},{24,28},{28,32},{32,36}... | collective-permute-start | bytes 3538952 | tf_op jit(solution)/shard_map/ppermute | solution.py:15
  263.2 64.0 %collective-permute-start.3 = (bf16[384,1536]{1,0:T(8,128)(2,1)}, bf16[384,1536]{1,0:T(8,128)(2,1)}, u32[]{:S(2)}, u32[]{:S(2)}) collective-permute-start(bf16[384,1536]{1,0:T(8,128)(2,1)} %pad_maximum_fusion.3), channel_id=1, source_target_pairs={{4,0},{8,4},{12,8},{16,12},{20,16},{24,20},{28,24},{32,28},{36,32}... | collective-permute-start | bytes 3538952 | tf_op jit(solution)/shard_map/ppermute | solution.py:15
  268.6 55.1 %all-to-all-start.4 = ((bf16[4,96,768]{2,1,0:T(8,128)(2,1)}), bf16[4,96,768]{2,1,0:T(8,128)(2,1)}, u32[]{:S(2)}, u32[]{:S(2)}) async-start(bf16[4,96,768]{2,1,0:T(8,128)(2,1)} %bitcast.162), calls=%async_computation.4 | async-start | bytes 1179648 | tf_op jit(solution)/shard_map/all_to_all | solution.py:136
  323.7 13.0 %all-to-all-start.5 = ((bf16[4,96,768]{2,1,0:T(8,128)(2,1)}), bf16[4,96,768]{2,1,0:T(8,128)(2,1)S(1)}, u32[]{:S(2)}, u32[]{:S(2)}) async-start(bf16[4,96,768]{2,1,0:T(8,128)(2,1)} %bitcast.163), calls=%async_computation.5 | async-start | bytes 1179648 | tf_op jit(solution)/shard_map/all_to_all | solution.py:137
  348.5 13.0 %all-to-all-start.7 = ((bf16[4,96,768]{2,1,0:T(8,128)(2,1)}), bf16[4,96,768]{2,1,0:T(8,128)(2,1)S(1)}, u32[]{:S(2)}, u32[]{:S(2)}) async-start(bf16[4,96,768]{2,1,0:T(8,128)(2,1)} %bitcast.46), calls=%async_computation.7 | async-start | bytes 1179648 | tf_op jit(solution)/shard_map/all_to_all | solution.py:139
where the time goes:
time: 365 us; the launch traced here: 362 us
  waiting for transfers between devices  127 us (35%)
  local copies, waits for them, and re-layouts  98.8 us (27%)
  matrix products  53.6 us (15%)
  starting transfers between devices  36.4 us (10%)
  blocking collectives  23.9 us (7%)
  other arithmetic  22.1 us (6%)
    all_to_all x1, waiting for transfers between devices, per_device(): lax.all_to_all(query_in, 'head', split_axis=1, concat_axis=0, tiled=True)  51.1 us
    all_to_all x1, waiting for transfers between devices, per_device(): lax.all_to_all(attended, 'head', split_axis=0, concat_axis=1, tiled=True)  45.8 us
    broadcast_in_dim x12, local copies, waits for them, and re-layouts, per_device(): lax.map(per_tile, (query_tiles, grad_tiles, neighbours))  20 us
    dot_general x6, matrix products, attend_tile(): jnp.einsum('hqk,khd->qhd', weights_low, val_heads, preferred_element_type...  18.4 us
    ppermute x4, starting transfers between devices, shifted(): return lax.ppermute(shard, axis, pairs)  14.7 us
    dynamic_slice x12, local copies, waits for them, and re-layouts, per_device(): lax.map(per_tile, (query_tiles, grad_tiles, neighbours))  14.6 us
    all_to_all x1, blocking collectives, per_device(): lax.all_to_all(value_in, 'head', split_axis=1, concat_axis=0, tiled=True)  12 us
    all_to_all x1, blocking collectives, per_device(): lax.all_to_all(grad_key, 'head', split_axis=0, concat_axis=1, tiled=True)  11.9 us
  transfers between devices with their start and end apart: 10, of which 6 were waited for; matrix products, arithmetic and copies ran while one was open for 6% of the time, Pallas kernels for 0%

commit v1 on v0

v1 whole, which is shorter than its diff:
```python
import functools
import math

import jax
import jax.numpy as jnp
from jax import lax
from jax.experimental import pallas as pl
from jax.experimental.pallas import tpu as pltpu
from jax.sharding import PartitionSpec as P

HD = 128
TILE = 64
MESH = pl.DeviceIdType.MESH
F32 = jnp.float32
BF16 = jnp.bfloat16
NEG = -1e30

NN = (((1,), (0,)), ((), ()))
NT = (((1,), (1,)), ((), ()))
TN = (((0,), (0,)), ((), ()))


def dot(a, b, dims):
    return lax.dot_general(a, b, dims, preferred_element_type=F32)


def attend_head(i, kv, qd, bias, s_scr, p_scr, d_scr, own32, near32, far16, outs):
    rows = qd.shape[2]
    tiles = rows // TILE
    scale = 1.0 / math.sqrt(HD)
    c = scale * math.log2(math.e)
    query = qd[i, 0]
    peak = None
    for b in range(3):
        s = dot(kv[b, i, 0], query, NT)
        s = s.reshape(tiles, TILE // 8, 8, rows) + bias[b * tiles : (b + 1) * tiles][:, None]
        top = jnp.max(s, axis=(0, 1))
        peak = top if peak is None else jnp.maximum(peak, top)
        s_scr[b * rows : (b + 1) * rows] = s.reshape(rows, rows)
    peak = jnp.max(peak, axis=0, keepdims=True)
    total = None
    out_t = None
    for b in range(3):
        part = slice(b * rows, (b + 1) * rows)
        e = jnp.exp2((s_scr[part] - peak) * c)
        t = jnp.sum(e.reshape(rows // 8, 8, rows), axis=0)
        total = t if total is None else total + t
        low = e.astype(BF16)
        p_scr[part] = low
        s_scr[part] = e
        o = dot(kv[b, i, 1], low, TN)
        out_t = o if out_t is None else out_t + o
    inv = 1.0 / jnp.sum(total, axis=0, keepdims=True)
    out_low = (out_t * inv).astype(BF16).astype(F32)
    outs[0, i] = out_low.T.astype(BF16)
    grad_t = qd[i, 1].astype(F32).T * inv
    grad_n = grad_t.T.astype(BF16)
    delta = jnp.sum(grad_t * out_low, axis=0, keepdims=True)
    dq_t = None
    for b in range(3):
        part = slice(b * rows, (b + 1) * rows)
        dp = dot(kv[b, i, 1], grad_n, NT)
        ds = (s_scr[part] * (dp - delta)).astype(BF16)
        dk = dot(ds, query, NN) * scale
        dv = dot(p_scr[part], grad_n, NN)
        if b == 2:
            far16[i, 0] = dk.astype(BF16)
            far16[i, 1] = dv.astype(BF16)
        else:
            held = own32 if b == 0 else near32
            held[i, 0] = dk
            held[i, 1] = dv
        g = dot(kv[b, i, 0], ds, TN)
        dq_t = g if dq_t is None else dq_t + g
    outs[1, i] = (dq_t * scale).T.astype(BF16)


def kernel(n, nbr, q, k, v, do, o_att, o_dq, o_dk, o_dv,
           kv, qd, bias, s_scr, p_scr, d_scr, own32, near32, far16, near16, gfar, gnear, outs,
           kv_in, qd_in, kv_out, qd_out, sa, ra, sb, rb, sc, rc, sd, rd, so, ro, lo):
    block = q.shape[0]
    rows = qd.shape[2]
    heads = qd.shape[0]
    tiles = rows // TILE
    width = heads * HD
    s = lax.axis_index("slab")
    h = lax.axis_index("head")
    odd = lax.rem(s, 2)
    near = s + 1 - 2 * odd
    onward = lax.rem(s + 2 - 4 * odd + n, n)
    source = lax.rem(s - 2 + 4 * odd + n, n)
    across = lax.rem(h + 2, 4)
    beside = h + 1 - 2 * lax.rem(h, 2)
    slab_peers = (s, lax.rem(beside + 2, 4)), (s, across), (s, beside)
    near_id, onward_id, source_id = (near, across), (onward, h), (source, h)

    def group(head):
        return lax.rem(head + 2 * odd, 4)

    def columns(head, i):
        return pl.ds(pl.multiple_of(group(head) * width + i * HD, HD), HD)

    def block_of(head):
        return pl.ds(pl.multiple_of(head * block, 32), block)

    barrier = pltpu.get_barrier_semaphore()
    for peer in slab_peers + (near_id, onward_id, source_id):
        pl.semaphore_signal(barrier, inc=1, device_id=peer, device_id_type=MESH)

    lane_tile = lax.broadcasted_iota(jnp.int32, (8, rows), 1) // TILE
    far_first = jnp.where(s == 0, -1000, (s - 1 + 2 * odd) * tiles)
    firsts = (s * tiles, near * tiles, far_first)
    listed = []
    for slot in range(nbr.shape[1]):
        row = jnp.full((8, rows), nbr[0, slot], jnp.int32)
        for t in range(1, tiles):
            row = jnp.where(lane_tile == t, nbr[t, slot], row)
        listed.append(row)
    for b in range(3):
        for t in range(tiles):
            hit = listed[0] == firsts[b] + t
            for row in listed[1:]:
                hit = hit | (row == firsts[b] + t)
            bias[b * tiles + t] = jnp.where(hit, 0.0, NEG)

    pl.semaphore_wait(barrier, 6)

    def send(src, dst, s_sem, r_sem, peer):
        pltpu.make_async_remote_copy(
            src_ref=src, dst_ref=dst, send_sem=s_sem, recv_sem=r_sem,
            device_id=peer, device_id_type=MESH,
        ).start()

    def arrive(ref, sem):
        pltpu.make_async_copy(ref, ref, sem).wait()

    def spread(i, pair, into, s_sem, r_sem):
        for peer in slab_peers:
            for a, ref in enumerate(pair):
                send(ref.at[:, columns(peer[1], i)], into.at[i, a, block_of(h), :],
                     s_sem.at[i], r_sem.at[i], peer)
        for a, ref in enumerate(pair):
            pltpu.make_async_copy(
                ref.at[:, columns(h, i)], into.at[i, a, block_of(h), :], r_sem.at[i]
            ).start()

    own = kv.at[0]

    @pl.loop(0, heads)
    def _(i):
        spread(i, (k, v), own, kv_out, kv_in)

    @pl.loop(0, heads)
    def _(i):
        spread(i, (q, do), qd, qd_out, qd_in)

    def gather(i, a, out, r):
        for peer in slab_peers:
            send(outs.at[a, i, block_of(peer[1]), :], out.at[:, columns(h, i)],
                 so.at[a], ro.at[a], peer)
        pltpu.make_async_copy(
            outs.at[a, i, block_of(h), :], out.at[:, columns(h, i)], lo.at[a]
        ).start()

    def ship(i):
        arrive(kv.at[0, i], kv_in.at[i])
        send(kv.at[0, i], kv.at[1, i], sa.at[i], ra.at[i], near_id)

    def relay(i):
        arrive(kv.at[1, i], ra.at[i])
        send(kv.at[1, i], kv.at[2, i], sb.at[i], rb.at[i], onward_id)

    def compute(i):
        arrive(kv.at[2, i], rb.at[i])
        arrive(qd.at[i], qd_in.at[i])
        attend_head(i, kv, qd, bias, s_scr, p_scr, d_scr, own32, near32, far16, outs)
        send(far16.at[i], gfar.at[i], sc.at[i], rc.at[i], source_id)
        gather(i, 0, o_att, 0)
        gather(i, 1, o_dq, 1)

    def fold(i):
        arrive(gfar.at[i], rc.at[i])
        near16[i] = (near32[i] + gfar[i].astype(F32)).astype(BF16)
        send(near16.at[i], gnear.at[i], sd.at[i], rd.at[i], near_id)

    def finish(i):
        arrive(gnear.at[i], rd.at[i])
        done = (own32[i] + gnear[i].astype(F32)).astype(BF16)
        outs[2, i] = done[0]
        outs[3, i] = done[1]
        gather(i, 2, o_dk, 2)
        gather(i, 3, o_dv, 3)

    ship(0)
    ship(1)

    @pl.loop(0, heads + 5)
    def _(step):
        for lag, task in ((-2, ship), (0, relay), (5, finish), (3, fold), (1, compute)):
            i = step - lag

            @pl.when((i >= (2 if lag < 0 else 0)) & (i < heads))
            def _():
                task(i)

    for i in range(heads):
        arrive(kv.at[0, i, :, 0 : 3 * block], kv_out.at[i])
        arrive(qd.at[i, :, 0 : 3 * block], qd_out.at[i])
        arrive(kv.at[0, i], sa.at[i])
        arrive(kv.at[1, i], sb.at[i])
        arrive(far16.at[i], sc.at[i])
        arrive(near16.at[i], sd.at[i])
    for a in range(4):
        arrive(outs.at[a, :, 0 : 3 * block], so.at[a])
        arrive(outs.at[a, :, 0 : 3 * block], ro.at[a])
        arrive(outs.at[a, :, 0:block], lo.at[a])


def solution(mesh):
    n = mesh.shape["slab"]
    parts = mesh.shape["head"]

    def step(query_in, key_in, value_in, grad_out, neighbours):
        block, full = query_in.shape
        rows = block * parts
        heads = full // parts // HD
        tiles = rows // TILE
        shape = jax.ShapeDtypeStruct((block, full), BF16)
        pair16 = pltpu.VMEM((heads, 2, rows, HD), BF16)
        pair32 = pltpu.VMEM((heads, 2, rows, HD), F32)
        each = pltpu.SemaphoreType.DMA((heads,))
        four = pltpu.SemaphoreType.DMA((4,))
        return pl.pallas_call(
            functools.partial(kernel, n),
            out_shape=(shape,) * 4,
            in_specs=[pl.BlockSpec(memory_space=pltpu.SMEM)]
            + [pl.BlockSpec(memory_space=pl.ANY)] * 4,
            out_specs=(pl.BlockSpec(memory_space=pl.ANY),) * 4,
            scratch_shapes=[
                pltpu.VMEM((3, heads, 2, rows, HD), BF16),
                pair16,
                pltpu.VMEM((3 * tiles, 8, rows), F32),
                pltpu.VMEM((3 * rows, rows), F32),
                pltpu.VMEM((3 * rows, rows), BF16),
                pltpu.VMEM((8, HD), BF16),
                pair32, pair32,
                pair16, pair16, pair16, pair16,
                pltpu.VMEM((4, heads, rows, HD), BF16),
            ] + [each] * 12 + [four] * 3,
            compiler_params=pltpu.CompilerParams(
                collective_id=0, has_side_effects=True, vmem_limit_bytes=60 * 1024 * 1024
            ),
        )(neighbours, query_in, key_in, value_in, grad_out)

    rows_spec = P(("slab", "head"), None)
    return jax.shard_map(
        step, mesh=mesh, in_specs=(rows_spec,) * 4 + (P("slab", None),),
        out_specs=(rows_spec,) * 4, check_vma=False,
    )
```

time: 365 us -> 82.1 us (0.22)
  the two profiles are of different devices: /device:TPU:22 before, /device:TPU:1 now
where the time goes in v1:
time: 82.1 us; the launch traced here: 81.8 us
  Pallas kernels  75.8 us (92%)
  local copies, waits for them, and re-layouts  5.35 us (7%)
    pallas_call x1, Pallas kernels, step(): pl.pallas_call(functools.partial(kernel, n), out_shape=(shape,) * 4, in_s...  75.8 us
    unnamed x10, local copies, waits for them, and re-layouts  5.35 us

profile of v1, /device:TPU:1, one launch (start us, length us, event | category | flops | bytes accessed | tf_op | source)
XLA Modules:
  0.0 81.8 jit_solution(8426241853194340124)
XLA Ops:
  0.6 75.8 %shard_map.84 = (bf16[96,3072]{1,0:T(8,128)(2,1)}, bf16[96,3072]{1,0:T(8,128)(2,1)}, bf16[96,3072]{1,0:T(8,128)(2,1)}, bf16[96,3072]{1,0:T(8,128)(2,1)}) custom-call(s32[6,16]{1,0:T(8,128)} %nbr.1, bf16[96,3072]{1,0:T(8,128)(2,1)} %q.1, bf16[96,3072]{1,0:T(8,128)(2,1)} %k.1, bf16[96,3072]{1,0:T(8,128)(2,1)} %v.1, bf16[96,3072]{1,0:T(8,128)(2,1)} %do.1), custom_call_target="tpu_custom_call" | custom-call | tf_op jit(solution)/shard_map/pallas_call | solution.py:233
  76.5 0.0 copy-start.2
  76.5 2.0 %copy.13 = bf16[96,3072]{1,0:T(8,128)(2,1)} copy(bf16[96,3072]{1,0:T(8,128)(2,1)} %get-tuple-element.8) | data formatting | bytes 1179648
  78.4 0.0 copy-done.2
  78.5 0.0 copy-start.1
  78.5 0.8 copy.14
  79.3 0.5 copy-done.1
  79.7 0.0 copy-start
  79.7 0.8 copy.15
  80.5 0.5 copy-done
  81.0 0.8 copy.16
Async XLA Ops:
  76.5 2.0 %copy-start.2 = (bf16[96,3072]{1,0:T(8,128)(2,1)S(1)}, bf16[96,3072]{1,0:T(8,128)(2,1)}, u32[]{:S(2)}) copy-start(bf16[96,3072]{1,0:T(8,128)(2,1)} %get-tuple-element.9) | copy-start | bytes 1769476
  78.5 1.3 %copy-start.1 = (bf16[96,3072]{1,0:T(8,128)(2,1)S(1)}, bf16[96,3072]{1,0:T(8,128)(2,1)}, u32[]{:S(2)}) copy-start(bf16[96,3072]{1,0:T(8,128)(2,1)} %get-tuple-element.10) | copy-start | bytes 1769476
  79.7 1.3 %copy-start = (bf16[96,3072]{1,0:T(8,128)(2,1)S(1)}, bf16[96,3072]{1,0:T(8,128)(2,1)}, u32[]{:S(2)}) copy-start(bf16[96,3072]{1,0:T(8,128)(2,1)} %get-tuple-element.11) | copy-start | bytes 1769476

commit v2 on v1

v2 whole, which is shorter than its diff:
```python
import functools
import math

import jax
import jax.numpy as jnp
from jax import lax
from jax.experimental import pallas as pl
from jax.experimental.pallas import tpu as pltpu
from jax.sharding import PartitionSpec as P

HD = 128
TILE = 64
MESH = pl.DeviceIdType.MESH
F32 = jnp.float32
BF16 = jnp.bfloat16
NEG = -1e30

NN = (((1,), (0,)), ((), ()))
NT = (((1,), (1,)), ((), ()))
TN = (((0,), (0,)), ((), ()))


def dot(a, b, dims):
    return lax.dot_general(a, b, dims, preferred_element_type=F32)


def attend_head(i, kv, qd, bias, s_scr, p_scr, own32, near32, far16, outs):
    rows = qd.shape[2]
    tiles = rows // TILE
    scale = 1.0 / math.sqrt(HD)
    c = scale * math.log2(math.e)
    query = qd[i, 0]
    peak = None
    for b in range(3):
        s = dot(kv[b, i, 0], query, NT)
        s = s.reshape(tiles, TILE // 8, 8, rows) + bias[b * tiles : (b + 1) * tiles][:, None]
        top = jnp.max(s, axis=(0, 1))
        peak = top if peak is None else jnp.maximum(peak, top)
        s_scr[b * rows : (b + 1) * rows] = s.reshape(rows, rows)
    peak = jnp.max(peak, axis=0, keepdims=True)
    total = None
    out_t = None
    for b in range(3):
        part = slice(b * rows, (b + 1) * rows)
        e = jnp.exp2((s_scr[part] - peak) * c)
        t = jnp.sum(e.reshape(rows // 8, 8, rows), axis=0)
        total = t if total is None else total + t
        low = e.astype(BF16)
        p_scr[part] = low
        s_scr[part] = e
        o = dot(kv[b, i, 1], low, TN)
        out_t = o if out_t is None else out_t + o
    inv = 1.0 / jnp.sum(total, axis=0, keepdims=True)
    out_low = (out_t * inv).astype(BF16).astype(F32)
    outs[0, i] = out_low.T.astype(BF16)
    grad_t = qd[i, 1].astype(F32).T * inv
    grad_n = grad_t.T.astype(BF16)
    delta = jnp.sum(grad_t * out_low, axis=0, keepdims=True)
    dq_t = None
    for b in range(3):
        part = slice(b * rows, (b + 1) * rows)
        dp = dot(kv[b, i, 1], grad_n, NT)
        ds = (s_scr[part] * (dp - delta)).astype(BF16)
        dk = dot(ds, query, NN) * scale
        dv = dot(p_scr[part], grad_n, NN)
        if b == 2:
            far16[i, 0] = dk.astype(BF16)
            far16[i, 1] = dv.astype(BF16)
        else:
            held = own32 if b == 0 else near32
            held[i, 0] = dk
            held[i, 1] = dv
        g = dot(kv[b, i, 0], ds, TN)
        dq_t = g if dq_t is None else dq_t + g
    outs[1, i] = (dq_t * scale).T.astype(BF16)


def kernel(n, listing, q, k, v, do, o_att, o_dq, o_dk, o_dv,
           kv, qd, bias, s_scr, p_scr, own32, near32, far16, near16, gfar, gnear, outs,
           kv_own, kv_beside, kv_cross, kv_out, qd_in, qd_out,
           sa, ra, sb, rb, sc, rc, sd, rd, so, ro, lo, ready, nbr, nbr_in):
    block = q.shape[0]
    rows = qd.shape[2]
    heads = qd.shape[0]
    tiles = rows // TILE
    width = heads * HD
    s = lax.axis_index("slab")
    h = lax.axis_index("head")
    odd = lax.rem(s, 2)
    near = s + 1 - 2 * odd
    above = lax.rem(s + 2, n)
    below = lax.rem(s - 2 + n, n)
    onward = jnp.where(odd == 0, above, below)
    source = jnp.where(odd == 0, below, above)
    across = lax.rem(h + 2, 4)
    beside = h + 1 - 2 * lax.rem(h, 2)
    slab_peers = (s, across), (s, lax.rem(beside + 2, 4)), (s, beside)
    near_id, onward_id, source_id = (near, across), (onward, h), (source, h)
    depth = min(16, n // 2)
    level = lax.rem(s // 2, depth)
    first = jnp.where(level == 0, 1, 0)
    last = jnp.where(level == depth - 1, 1, 0)

    def group(head):
        return lax.rem(head + 2 * odd, 4)

    def columns(head, i):
        return pl.ds(pl.multiple_of(group(head) * width + i * HD, HD), HD)

    def block_of(head):
        return pl.ds(pl.multiple_of(head * block, 32), block)

    cross_rows = pl.ds(pl.multiple_of((1 - h // 2) * (2 * block), 32), 2 * block)

    def signal(sem, peer):
        pl.semaphore_signal(sem, inc=1, device_id=peer, device_id_type=MESH)

    barrier = pltpu.get_barrier_semaphore()
    for peer in slab_peers + (near_id,):
        signal(barrier, peer)

    @pl.when(last == 0)
    def _():
        signal(barrier, (above, h))

    @pl.when(first == 1)
    def _():
        signal(barrier, (below, h))

    pl.semaphore_wait(barrier, 5 - first + last)

    def send(src, dst, s_sem, r_sem, peer):
        pltpu.make_async_remote_copy(
            src_ref=src, dst_ref=dst, send_sem=s_sem, recv_sem=r_sem,
            device_id=peer, device_id_type=MESH,
        ).start()

    def arrive(ref, sem):
        pltpu.make_async_copy(ref, ref, sem).wait()

    def spread(i, pair, into, out, sems, mine):
        for peer, sem in zip(slab_peers, sems):
            for a, ref in enumerate(pair):
                send(ref.at[:, columns(peer[1], i)], into.at[i, a, block_of(h), :],
                     out.at[i], sem.at[i], peer)
        for a, ref in enumerate(pair):
            pltpu.make_async_copy(
                ref.at[:, columns(h, i)], into.at[i, a, block_of(h), :], mine.at[i]
            ).start()

    def spread_kv(i):
        spread(i, (k, v), kv.at[0], kv_out, (kv_cross, kv_cross, kv_beside), kv_own)

    def spread_qd(i):
        spread(i, (q, do), qd, qd_out, (qd_in, qd_in, qd_in), qd_in)

    def ship_held(i):
        for a, ref in enumerate((k, v)):
            send(ref.at[:, columns(h, i)], kv.at[1, i, a, block_of(h), :], sa.at[i], ra.at[i], near_id)

    def ship_beside(i):
        part = kv.at[0, i, :, block_of(beside), :]
        arrive(part, kv_beside.at[i])
        send(part, kv.at[1, i, :, block_of(beside), :], sa.at[i], ra.at[i], near_id)

    def ship_cross(i):
        part = kv.at[0, i, :, cross_rows, :]
        arrive(part, kv_cross.at[i])
        send(part, kv.at[1, i, :, cross_rows, :], sa.at[i], ra.at[i], near_id)

    def gather(i, a, out):
        for peer in slab_peers:
            send(outs.at[a, i, block_of(peer[1]), :], out.at[:, columns(h, i)],
                 so.at[a], ro.at[a], peer)
        pltpu.make_async_copy(
            outs.at[a, i, block_of(h), :], out.at[:, columns(h, i)], lo.at[a]
        ).start()

    def relay(i):
        arrive(kv.at[1, i], ra.at[i])
        send(kv.at[1, i], kv.at[2, i], sb.at[i], rb.at[i], onward_id)

    def compute(i):
        arrive(kv.at[0, i, :, block_of(h), :], kv_own.at[i])
        arrive(qd.at[i], qd_in.at[i])
        arrive(kv.at[2, i], rb.at[i])
        attend_head(i, kv, qd, bias, s_scr, p_scr, own32, near32, far16, outs)

        @pl.when((i == 0) & (jnp.where(odd == 0, first, 1 - last) == 1))
        def _():
            pl.semaphore_wait(ready.at[1], 1)

        send(far16.at[i], gfar.at[i], sc.at[i], rc.at[i], source_id)
        gather(i, 0, o_att)
        gather(i, 1, o_dq)

    def fold(i):
        arrive(gfar.at[i], rc.at[i])
        for a in range(2):
            near16[i, a] = (near32[i, a] + gfar[i, a].astype(F32)).astype(BF16)
            send(near16.at[i, a], gnear.at[i, a], sd.at[i], rd.at[i, a], near_id)

    def finish(i):
        for a, out in enumerate((o_dk, o_dv)):
            arrive(gnear.at[i, a], rd.at[i, a])
            outs[2 + a, i] = (own32[i, a] + gnear[i, a].astype(F32)).astype(BF16)
            gather(i, 2 + a, out)

    def ship_on(i):
        ship_cross(i)

        @pl.when(i + 1 < heads)
        def _():
            ship_held(i + 1)
            ship_beside(i + 1)

    listing_copy = pltpu.make_async_copy(listing, nbr, nbr_in)
    listing_copy.start()

    spread_kv(0)
    ship_held(0)
    spread_kv(1)
    ship_held(1)
    spread_kv(2)
    for i in range(3, heads):
        spread_qd(i - 3)
        spread_kv(i)
    for i in range(max(heads - 3, 0), heads):
        spread_qd(i)

    @pl.when(first == 0)
    def _():
        signal(ready.at[odd], (below, h))

    @pl.when(last == 1)
    def _():
        signal(ready.at[1 - odd], (above, h))

    ship_beside(0)
    ship_beside(1)

    listing_copy.wait()
    lane_tile = lax.broadcasted_iota(jnp.int32, (8, rows), 1) // TILE
    far_first = jnp.where(s == 0, -1000, (s - 1 + 2 * odd) * tiles)
    firsts = (s * tiles, near * tiles, far_first)
    listed = []
    for slot in range(nbr.shape[1]):
        row = jnp.full((8, rows), nbr[0, slot], jnp.int32)
        for t in range(1, tiles):
            row = jnp.where(lane_tile == t, nbr[t, slot], row)
        listed.append(row)
    for b in range(3):
        for t in range(tiles):
            hit = listed[0] == firsts[b] + t
            for row in listed[1:]:
                hit = hit | (row == firsts[b] + t)
            bias[b * tiles + t] = jnp.where(hit, 0.0, NEG)

    ship_cross(0)
    ship_on(1)

    @pl.when(jnp.where(odd == 0, 1 - last, first) == 1)
    def _():
        pl.semaphore_wait(ready.at[0], 1)

    relay(0)
    ship_on(2)

    hold = 2 * first * (1 - odd)
    turn = first * odd

    @pl.loop(0, heads + 6)
    def _(step):
        for start, lag, task in ((1, -1, relay), (3, -3, ship_on), (0, 3 + turn, fold), (0, hold, compute), (0, 6, finish)):
            i = step - lag

            @pl.when((i >= start) & (i < heads))
            def _():
                task(i)

    for i in range(heads):
        arrive(kv.at[0, i, :, 0 : 3 * block], kv_out.at[i])
        arrive(qd.at[i, :, 0 : 3 * block], qd_out.at[i])
        arrive(kv.at[0, i], sa.at[i])
        arrive(kv.at[1, i], sb.at[i])
        arrive(far16.at[i], sc.at[i])
        arrive(near16.at[i], sd.at[i])
    for a in range(4):
        arrive(outs.at[a, :, 0 : 3 * block], so.at[a])
        arrive(outs.at[a, :, 0 : 3 * block], ro.at[a])
        arrive(outs.at[a, :, 0:block], lo.at[a])


def solution(mesh):
    n = mesh.shape["slab"]
    parts = mesh.shape["head"]

    def step(query_in, key_in, value_in, grad_out, neighbours):
        block, full = query_in.shape
        rows = block * parts
        heads = full // parts // HD
        tiles = rows // TILE
        shape = jax.ShapeDtypeStruct((block, full), BF16)
        pair16 = pltpu.VMEM((heads, 2, rows, HD), BF16)
        pair32 = pltpu.VMEM((heads, 2, rows, HD), F32)
        each = pltpu.SemaphoreType.DMA((heads,))
        four = pltpu.SemaphoreType.DMA((4,))
        held = pl.pallas_call(
            functools.partial(kernel, n),
            out_shape=(pltpu.VMEM((block, full), BF16),) * 4,
            in_specs=[pl.BlockSpec(memory_space=pl.ANY)] * 5,
            out_specs=(pl.BlockSpec(memory_space=pltpu.VMEM),) * 4,
            scratch_shapes=[
                pltpu.VMEM((3, heads, 2, rows, HD), BF16),
                pair16,
                pltpu.VMEM((3 * tiles, 8, rows), F32),
                pltpu.VMEM((3 * rows, rows), F32),
                pltpu.VMEM((3 * rows, rows), BF16),
                pair32, pair32,
                pair16, pair16, pair16, pair16,
                pltpu.VMEM((4, heads, rows, HD), BF16),
            ] + [each] * 13 + [pltpu.SemaphoreType.DMA((heads, 2))] + [four] * 3
            + [pltpu.SemaphoreType.REGULAR((2,)), pltpu.SMEM(neighbours.shape, jnp.int32),
               pltpu.SemaphoreType.DMA],
            compiler_params=pltpu.CompilerParams(
                collective_id=0, has_side_effects=True, vmem_limit_bytes=61 * 1024 * 1024 + 512 * 1024
            ),
        )(neighbours, query_in, key_in, value_in, grad_out)
        return held

    rows_spec = P(("slab", "head"), None)
    return jax.shard_map(
        step, mesh=mesh, in_specs=(rows_spec,) * 4 + (P("slab", None),),
        out_specs=(rows_spec,) * 4, check_vma=False,
    )
```

time: 82.1 us -> 73 us (0.89)
  Pallas kernels: 75.8 us -> 69 us
  local copies, waits for them, and re-layouts: 5.35 us -> 3.26 us
    pallas_call x1, Pallas kernels: 75.8 us -> 69 us  [step(): pl.pallas_call(functools.partial(kernel, n), out_shape=(pltpu.VMEM((block...]
    unnamed x10 -> x4, local copies, waits for them, and re-layouts: 5.35 us -> 3.26 us
where the time goes in v2:
time: 73 us; the launch traced here: 72.9 us
  Pallas kernels  69 us (95%)
  local copies, waits for them, and re-layouts  3.26 us (4%)
    pallas_call x1, Pallas kernels, step(): pl.pallas_call(functools.partial(kernel, n), out_shape=(pltpu.VMEM((block...  69 us
    unnamed x4, local copies, waits for them, and re-layouts  3.26 us

profile of v2, /device:TPU:1, one launch (start us, length us, event | category | flops | bytes accessed | tf_op | source)
XLA Modules:
  0.0 72.9 jit_solution(15067411456989230379)
XLA Ops:
  0.6 69.0 %shard_map.84 = (bf16[96,3072]{1,0:T(8,128)(2,1)S(1)}, bf16[96,3072]{1,0:T(8,128)(2,1)S(1)}, bf16[96,3072]{1,0:T(8,128)(2,1)S(1)}, bf16[96,3072]{1,0:T(8,128)(2,1)S(1)}) custom-call(s32[6,16]{1,0:T(8,128)} %listing.1, bf16[96,3072]{1,0:T(8,128)(2,1)} %q.1, bf16[96,3072]{1,0:T(8,128)(2,1)} %k.1, bf16[96,3072]{1,0:T(8,128)(2,1)} %v.1, bf16[96,3072]{1,0:T(8,128)(2,1)} %do.1), custom_call_target="tpu_custom_call" | custom-call | tf_op jit(solution)/shard_map/pallas_call | solution.py:308
  69.6 0.8 %copy.13 = bf16[96,3072]{1,0:T(8,128)(2,1)} copy(bf16[96,3072]{1,0:T(8,128)(2,1)S(1)} %get-tuple-element.4) | data formatting | bytes 1179648
  70.4 0.8 %copy.14 = bf16[96,3072]{1,0:T(8,128)(2,1)} copy(bf16[96,3072]{1,0:T(8,128)(2,1)S(1)} %get-tuple-element.5) | data formatting | bytes 1179648
  71.2 0.8 %copy.15 = bf16[96,3072]{1,0:T(8,128)(2,1)} copy(bf16[96,3072]{1,0:T(8,128)(2,1)S(1)} %get-tuple-element.6) | data formatting | bytes 1179648
  72.0 0.8 %copy.16 = bf16[96,3072]{1,0:T(8,128)(2,1)} copy(bf16[96,3072]{1,0:T(8,128)(2,1)S(1)} %get-tuple-element.7) | data formatting | bytes 1179648

commit v3 on v2

--- a/solution.py
+++ b/solution.py
@@ -100,6 +100,8 @@
     level = lax.rem(s // 2, depth)
     first = jnp.where(level == 0, 1, 0)
     last = jnp.where(level == depth - 1, 1, 0)
+    lone = (s == 0) | (s == n - 1)
+    single = (s == 1) | (s == n - 2)
 
     def group(head):
         return lax.rem(head + 2 * odd, 4)
@@ -111,6 +113,7 @@
         return pl.ds(pl.multiple_of(head * block, 32), block)
 
     cross_rows = pl.ds(pl.multiple_of((1 - h // 2) * (2 * block), 32), 2 * block)
+    local_rows = pl.ds(pl.multiple_of((h // 2) * (2 * block), 32), 2 * block)
 
     def signal(sem, peer):
         pl.semaphore_signal(sem, inc=1, device_id=peer, device_id_type=MESH)
@@ -168,17 +171,25 @@
         arrive(part, kv_cross.at[i])
         send(part, kv.at[1, i, :, cross_rows, :], sa.at[i], ra.at[i], near_id)
 
-    def gather(i, a, out):
-        for peer in slab_peers:
+    def gather(i, a, out, peers, mine):
+        for peer in peers:
             send(outs.at[a, i, block_of(peer[1]), :], out.at[:, columns(h, i)],
                  so.at[a], ro.at[a], peer)
-        pltpu.make_async_copy(
-            outs.at[a, i, block_of(h), :], out.at[:, columns(h, i)], lo.at[a]
-        ).start()
+        if mine:
+            pltpu.make_async_copy(
+                outs.at[a, i, block_of(h), :], out.at[:, columns(h, i)], lo.at[a]
+            ).start()
 
     def relay(i):
         arrive(kv.at[1, i], ra.at[i])
-        send(kv.at[1, i], kv.at[2, i], sb.at[i], rb.at[i], onward_id)
+
+        @pl.when(jnp.logical_not(single))
+        def _():
+            send(kv.at[1, i], kv.at[2, i], sb.at[i], rb.at[i], onward_id)
+
+        @pl.when(lone)
+        def _():
+            pltpu.make_async_copy(kv.at[1, i], kv.at[2, i], rb.at[i]).start()
 
     def compute(i):
         arrive(kv.at[0, i, :, block_of(h), :], kv_own.at[i])
@@ -186,25 +197,48 @@
         arrive(kv.at[2, i], rb.at[i])
         attend_head(i, kv, qd, bias, s_scr, p_scr, own32, near32, far16, outs)
 
-        @pl.when((i == 0) & (jnp.where(odd == 0, first, 1 - last) == 1))
+        @pl.when((i == 0) & (jnp.where(odd == 0, first, 1 - last) == 1) & (s > 0))
         def _():
             pl.semaphore_wait(ready.at[1], 1)
 
-        send(far16.at[i], gfar.at[i], sc.at[i], rc.at[i], source_id)
-        gather(i, 0, o_att)
-        gather(i, 1, o_dq)
+        @pl.when(jnp.logical_not(lone))
+        def _():
+            for a in range(2):
+                send(far16.at[i, a], gfar.at[i, a], sc.at[i], rc.at[i, a], source_id)
+
+        gather(i, 0, o_att, slab_peers, True)
+        gather(i, 1, o_dq, slab_peers, True)
 
     def fold(i):
-        arrive(gfar.at[i], rc.at[i])
         for a in range(2):
-            near16[i, a] = (near32[i, a] + gfar[i, a].astype(F32)).astype(BF16)
-            send(near16.at[i, a], gnear.at[i, a], sd.at[i], rd.at[i, a], near_id)
+            @pl.when(jnp.logical_not(single))
+            def _():
+                arrive(gfar.at[i, a], rc.at[i, a])
+                near16[i, a] = (near32[i, a] + gfar[i, a].astype(F32)).astype(BF16)
+
+            @pl.when(single)
+            def _():
+                near16[i, a] = near32[i, a].astype(BF16)
+
+            if a == 0:
+                send(near16.at[i, a], gnear.at[i, a], sd.at[i], rd.at[i, a], near_id)
+            else:
+                for piece, part in ((1, local_rows), (2, cross_rows)):
+                    send(near16.at[i, a, part, :], gnear.at[i, a, part, :], sd.at[i], rd.at[i, piece], near_id)
+
+    def settle(i, a, part):
+        outs[2 + a, i, part, :] = (own32[i, a, part, :] + gnear[i, a, part, :].astype(F32)).astype(BF16)
 
     def finish(i):
-        for a, out in enumerate((o_dk, o_dv)):
-            arrive(gnear.at[i, a], rd.at[i, a])
-            outs[2 + a, i] = (own32[i, a] + gnear[i, a].astype(F32)).astype(BF16)
-            gather(i, 2 + a, out)
+        arrive(gnear.at[i, 0], rd.at[i, 0])
+        settle(i, 0, slice(None))
+        gather(i, 2, o_dk, slab_peers, True)
+        arrive(gnear.at[i, 1, cross_rows, :], rd.at[i, 1])
+        settle(i, 1, cross_rows)
+        gather(i, 3, o_dv, slab_peers[:2], False)
+        arrive(gnear.at[i, 1, local_rows, :], rd.at[i, 2])
+        settle(i, 1, local_rows)
+        gather(i, 3, o_dv, slab_peers[2:], True)
 
     def ship_on(i):
         ship_cross(i)
@@ -232,7 +266,7 @@
     def _():
         signal(ready.at[odd], (below, h))
 
-    @pl.when(last == 1)
+    @pl.when((last == 1) & (s < n - 2))
     def _():
         signal(ready.at[1 - odd], (above, h))
 
@@ -259,22 +293,22 @@
     ship_cross(0)
     ship_on(1)
 
-    @pl.when(jnp.where(odd == 0, 1 - last, first) == 1)
+    @pl.when((jnp.where(odd == 0, 1 - last, first) == 1) & (s != 1))
     def _():
         pl.semaphore_wait(ready.at[0], 1)
 
     relay(0)
     ship_on(2)
 
-    hold = 2 * first * (1 - odd)
-    turn = first * odd
+    hold = jnp.where((s > 0) & (odd == 0), 2 * first, 0)
 
     @pl.loop(0, heads + 6)
     def _(step):
-        for start, lag, task in ((1, -1, relay), (3, -3, ship_on), (0, 3 + turn, fold), (0, hold, compute), (0, 6, finish)):
+        for start, lag, task, here in ((1, -1, relay, True), (3, -3, ship_on, last == 0), (0, 3, fold, True),
+                                       (0, hold, compute, True), (3, -3, ship_on, last == 1), (0, 6, finish, True)):
             i = step - lag
 
-            @pl.when((i >= start) & (i < heads))
+            @pl.when((i >= start) & (i < heads) & here)
             def _():
                 task(i)
 
@@ -282,9 +316,17 @@
         arrive(kv.at[0, i, :, 0 : 3 * block], kv_out.at[i])
         arrive(qd.at[i, :, 0 : 3 * block], qd_out.at[i])
         arrive(kv.at[0, i], sa.at[i])
-        arrive(kv.at[1, i], sb.at[i])
-        arrive(far16.at[i], sc.at[i])
         arrive(near16.at[i], sd.at[i])
+    @pl.when(jnp.logical_not(single))
+    def _():
+        for i in range(heads):
+            arrive(kv.at[1, i], sb.at[i])
+
+    @pl.when(jnp.logical_not(lone))
+    def _():
+        for i in range(heads):
+            arrive(far16.at[i], sc.at[i])
+
     for a in range(4):
         arrive(outs.at[a, :, 0 : 3 * block], so.at[a])
         arrive(outs.at[a, :, 0 : 3 * block], ro.at[a])
@@ -319,7 +361,8 @@
                 pair32, pair32,
                 pair16, pair16, pair16, pair16,
                 pltpu.VMEM((4, heads, rows, HD), BF16),
-            ] + [each] * 13 + [pltpu.SemaphoreType.DMA((heads, 2))] + [four] * 3
+            ] + [each] * 11 + [pltpu.SemaphoreType.DMA((heads, 2)), each]
+            + [pltpu.SemaphoreType.DMA((heads, 3))] + [four] * 3
             + [pltpu.SemaphoreType.REGULAR((2,)), pltpu.SMEM(neighbours.shape, jnp.int32),
                pltpu.SemaphoreType.DMA],
             compiler_params=pltpu.CompilerParams(

time: 73 us -> 69.3 us (0.949)
  Pallas kernels: 69 us -> 64.8 us
    pallas_call x1, Pallas kernels: 69 us -> 64.8 us  [step(): pl.pallas_call(functools.partial(kernel, n), out_shape=(pltpu.VMEM((block...]
where the time goes in v3:
time: 69.3 us; the launch traced here: 68.7 us
  Pallas kernels  64.8 us (94%)
  local copies, waits for them, and re-layouts  3.26 us (5%)
    pallas_call x1, Pallas kernels, step(): pl.pallas_call(functools.partial(kernel, n), out_shape=(pltpu.VMEM((block...  64.8 us
    unnamed x4, local copies, waits for them, and re-layouts  3.26 us

profile of v3, /device:TPU:1, one launch (start us, length us, event | category | flops | bytes accessed | tf_op | source)
XLA Modules:
  0.0 68.7 jit_solution(13966919213093717559)
XLA Ops:
  0.6 64.8 %shard_map.84 = (bf16[96,3072]{1,0:T(8,128)(2,1)S(1)}, bf16[96,3072]{1,0:T(8,128)(2,1)S(1)}, bf16[96,3072]{1,0:T(8,128)(2,1)S(1)}, bf16[96,3072]{1,0:T(8,128)(2,1)S(1)}) custom-call(s32[6,16]{1,0:T(8,128)} %listing.1, bf16[96,3072]{1,0:T(8,128)(2,1)} %q.1, bf16[96,3072]{1,0:T(8,128)(2,1)} %k.1, bf16[96,3072]{1,0:T(8,128)(2,1)} %v.1, bf16[96,3072]{1,0:T(8,128)(2,1)} %do.1), custom_call_target="tpu_custom_call" | custom-call | tf_op jit(solution)/shard_map/pallas_call | solution.py:350
  65.4 0.8 %copy.13 = bf16[96,3072]{1,0:T(8,128)(2,1)} copy(bf16[96,3072]{1,0:T(8,128)(2,1)S(1)} %get-tuple-element.4) | data formatting | bytes 1179648
  66.3 0.8 %copy.14 = bf16[96,3072]{1,0:T(8,128)(2,1)} copy(bf16[96,3072]{1,0:T(8,128)(2,1)S(1)} %get-tuple-element.5) | data formatting | bytes 1179648
  67.1 0.8 %copy.15 = bf16[96,3072]{1,0:T(8,128)(2,1)} copy(bf16[96,3072]{1,0:T(8,128)(2,1)S(1)} %get-tuple-element.6) | data formatting | bytes 1179648
  67.9 0.8 %copy.16 = bf16[96,3072]{1,0:T(8,128)(2,1)} copy(bf16[96,3072]{1,0:T(8,128)(2,1)S(1)} %get-tuple-element.7) | data formatting | bytes 1179648

commit v4 on v3

--- a/solution.py
+++ b/solution.py
@@ -302,10 +302,10 @@
 
     hold = jnp.where((s > 0) & (odd == 0), 2 * first, 0)
 
-    @pl.loop(0, heads + 6)
+    @pl.loop(0, heads + 4)
     def _(step):
         for start, lag, task, here in ((1, -1, relay, True), (3, -3, ship_on, last == 0), (0, 3, fold, True),
-                                       (0, hold, compute, True), (3, -3, ship_on, last == 1), (0, 6, finish, True)):
+                                       (0, hold, compute, True), (3, -3, ship_on, last == 1), (0, 4, finish, True)):
             i = step - lag
 
             @pl.when((i >= start) & (i < heads) & here)

time: 69.3 us -> 68.9 us (level)
  no operation moved by 1% of the time
where the time goes in v4:
time: 68.9 us; the launch traced here: 68.8 us
  Pallas kernels  64.9 us (94%)
  local copies, waits for them, and re-layouts  3.26 us (5%)
    pallas_call x1, Pallas kernels, step(): pl.pallas_call(functools.partial(kernel, n), out_shape=(pltpu.VMEM((block...  64.9 us
    unnamed x4, local copies, waits for them, and re-layouts  3.26 us

profile of v4, /device:TPU:1, one launch (start us, length us, event | category | flops | bytes accessed | tf_op | source)
XLA Modules:
  0.0 68.8 jit_solution(6664702595827592304)
XLA Ops:
  0.6 64.9 %shard_map.84 = (bf16[96,3072]{1,0:T(8,128)(2,1)S(1)}, bf16[96,3072]{1,0:T(8,128)(2,1)S(1)}, bf16[96,3072]{1,0:T(8,128)(2,1)S(1)}, bf16[96,3072]{1,0:T(8,128)(2,1)S(1)}) custom-call(s32[6,16]{1,0:T(8,128)} %listing.1, bf16[96,3072]{1,0:T(8,128)(2,1)} %q.1, bf16[96,3072]{1,0:T(8,128)(2,1)} %k.1, bf16[96,3072]{1,0:T(8,128)(2,1)} %v.1, bf16[96,3072]{1,0:T(8,128)(2,1)} %do.1), custom_call_target="tpu_custom_call" | custom-call | tf_op jit(solution)/shard_map/pallas_call | solution.py:350
  65.5 0.8 %copy.13 = bf16[96,3072]{1,0:T(8,128)(2,1)} copy(bf16[96,3072]{1,0:T(8,128)(2,1)S(1)} %get-tuple-element.4) | data formatting | bytes 1179648
  66.3 0.8 %copy.14 = bf16[96,3072]{1,0:T(8,128)(2,1)} copy(bf16[96,3072]{1,0:T(8,128)(2,1)S(1)} %get-tuple-element.5) | data formatting | bytes 1179648
  67.1 0.8 %copy.15 = bf16[96,3072]{1,0:T(8,128)(2,1)} copy(bf16[96,3072]{1,0:T(8,128)(2,1)S(1)} %get-tuple-element.6) | data formatting | bytes 1179648
  68.0 0.8 %copy.16 = bf16[96,3072]{1,0:T(8,128)(2,1)} copy(bf16[96,3072]{1,0:T(8,128)(2,1)S(1)} %get-tuple-element.7) | data formatting | bytes 1179648
